TPU v7x, 256 devices: a whole 4x4x8 slice. The times are simulated.
256 devices in a mesh: bl: 64 (over y, z, core), ch: 4 (over x).
Axes of the slice: x: 4, y: 4, z: 8, core: 2. Of those that a mesh axis runs over, the one named last changes fastest.
Arguments:
- facet_grid: bfloat16 [4, 64, 16, 1024], P(None, None, None, 'ch'), may hold values from -0.75 to 0.75
- kernel: bfloat16 [131072, 1024], P('bl', 'ch'), may hold values from -0.1875 to 0.1875
- tile_of: int32 [256], P('bl'), may hold values from 0 to 3
- observed: bfloat16 [64, 2, 131072], P('ch', None, 'bl'), may hold values from -6 to 6
- flags: int32 [64, 131072], P('ch', 'bl'), may hold values 0 or 1
- pairs: int32 [2, 131072], P(None, 'bl'), may hold values from 0 to 511, as said below
- solver_order: int32 [512], replicated, may hold values from 0 to 511, as said below
Outputs:
- gains: float32 [64, 16, 512], P('ch', None, 'bl')
Inputs may be any that keep to these rules, and one draw needn't show every extreme that they name: `solver_order`: each station appears once. `pairs`: for row r, with j = (r mod 2048) // 32, the first station is solver_order[8 * j + m] for some m below 8; the second station differs from the first.
All inputs are finite; a program needn't handle non-finite values. No bound on the sum of `flags` on one device may be relied on, other than what follows from the above.
Results may differ from a plain program's by a relative error of at most 0.013.
Values may be sent and summed in bfloat16 or wider, within the bound.
No kernel may reach another device: no remote copies, remote signals or barrier semaphores. Data moves between devices by JAX's collectives and lax.ppermute only.
A program may use at most 128 MiB of HBM per device.

v0:
```python
import jax
import jax.numpy as jnp
from jax import lax
from jax.sharding import PartitionSpec as P

S = 512
ND = 8
ITERS = 4


def extended(shard, sides, width):
    for axis, dim in sides:
        devices, length = (lax.axis_size(axis), shard.shape[dim])
        up = [(i, (i + 1) % devices) for i in range(devices - 1)]
        down = [(j, i) for i, j in up]
        last = lax.slice_in_dim(shard, length - width, length, axis=dim)
        initial = lax.slice_in_dim(shard, 0, width, axis=dim)
        before = lax.ppermute(last, axis, up)
        after = lax.ppermute(initial, axis, down)
        shard = jnp.concatenate([before, shard, after], axis=dim)
    return shard


def lookup(gain_flat, pick):
    return jnp.dot(
        gain_flat, pick, precision=lax.Precision.HIGHEST, preferred_element_type=jnp.float32
    )


def row_terms(model_vis, visible, far_gain, near_gain):
    channels = model_vis.shape[0]
    row_count = model_vis.shape[2]
    model_pair = model_vis.reshape(channels, ND, 2, row_count)
    model_re = model_pair[:, :, 0].astype(jnp.float32)
    model_im = model_pair[:, :, 1].astype(jnp.float32)
    far_pair = far_gain.reshape(channels, ND, 2, row_count)
    near_pair = near_gain.reshape(channels, ND, 2, row_count)
    far_re = far_pair[:, :, 0]
    far_im = far_pair[:, :, 1]
    near_re = near_pair[:, :, 0]
    near_im = near_pair[:, :, 1]
    prod_re = model_re * far_re + model_im * far_im
    prod_im = model_im * far_re - model_re * far_im
    pred_re = jnp.sum(near_re * prod_re - near_im * prod_im, axis=1)
    pred_im = jnp.sum(near_re * prod_im + near_im * prod_re, axis=1)
    resid_re = visible[:, 0].astype(jnp.float32) - pred_re
    resid_im = visible[:, 1].astype(jnp.float32) - pred_im
    cross_re = prod_re * resid_re[:, None, :] + prod_im * resid_im[:, None, :]
    cross_im = prod_re * resid_im[:, None, :] - prod_im * resid_re[:, None, :]
    power = prod_re * prod_re + prod_im * prod_im
    stacked = jnp.concatenate([cross_re, cross_im, power], axis=1)
    return stacked.reshape(channels * 3 * ND, row_count)


def update_gains(gain_shard, sum_re, sum_im, power):
    channels = gain_shard.shape[0]
    owned = gain_shard.shape[2]
    gain_pair = gain_shard.reshape(channels, ND, 2, owned)
    gain_re = gain_pair[:, :, 0]
    gain_im = gain_pair[:, :, 1]
    new_re = (sum_re + gain_re * power) / (power + 1.0)
    new_im = (sum_im + gain_im * power) / (power + 1.0)
    averaged = jnp.stack([(gain_re + new_re) * 0.5, (gain_im + new_im) * 0.5], axis=2).reshape(
        channels, 2 * ND, owned
    )
    padded = extended(averaged, (("ch", 0),), 1)
    total_channels = channels * lax.axis_size("ch")
    chan_index = lax.axis_index("ch") * channels + jnp.arange(channels, dtype=jnp.int32)
    has_left = (chan_index > 0).astype(jnp.float32)[:, None, None]
    has_right = (chan_index < total_channels - 1).astype(jnp.float32)[:, None, None]
    return (0.25 * has_left * padded[:-2] + 0.5 * padded[1:-1] + 0.25 * has_right * padded[2:]) / (
        0.5 + 0.25 * has_left + 0.25 * has_right
    )


def body(facet_grid, kernel, tile_of, observed, flags, pairs, solver_order):
    channels = observed.shape[0]
    row_count = observed.shape[2]
    cell_count = kernel.shape[1]
    tile_count = facet_grid.shape[0]
    block_count = tile_of.shape[0]
    block_rows = row_count // block_count
    tile_pick = (tile_of[:, None] == jnp.arange(tile_count, dtype=jnp.int32)[None, :]).astype(
        jnp.bfloat16
    )
    kernel_blocks = kernel.reshape(block_count, block_rows, cell_count)
    chosen = jnp.einsum(
        "bt,tckg->bckg", tile_pick, facet_grid, preferred_element_type=jnp.float32
    ).astype(jnp.bfloat16)
    partial_vis = jnp.einsum(
        "bckg,bvg->ckbv", chosen, kernel_blocks, preferred_element_type=jnp.float32
    )
    summed = lax.psum_scatter(
        partial_vis.reshape(channels * lax.axis_size("ch"), partial_vis.shape[1], row_count).astype(
            jnp.bfloat16
        ),
        "ch",
        scatter_dimension=0,
        tiled=True,
    ).astype(jnp.float32)
    kept_rows = (1 - flags).astype(jnp.float32)
    model_vis = (summed * kept_rows[:, None, :]).astype(jnp.bfloat16)
    visible = (observed.astype(jnp.float32) * kept_rows[:, None, :]).astype(jnp.bfloat16)
    inverse = jnp.zeros((S,), jnp.int32).at[solver_order].set(jnp.arange(S, dtype=jnp.int32))
    bl_count = lax.axis_size("bl")
    owned = S // bl_count
    station_ids = jnp.arange(S, dtype=jnp.int32)[:, None]
    packed = pairs.reshape(1, 2, row_count)
    model_vis, visible, packed = (
        lax.all_to_all(model_vis, "bl", split_axis=2, concat_axis=2, tiled=True),
        lax.all_to_all(visible, "bl", split_axis=2, concat_axis=2, tiled=True),
        lax.all_to_all(packed, "bl", split_axis=2, concat_axis=2, tiled=True),
    )
    first_slot = inverse[packed[0, 0]]
    second_slot = inverse[packed[0, 1]]
    owner_slot = first_slot - lax.axis_index("bl") * owned
    near_pick = (owner_slot[None, :] == jnp.arange(owned, dtype=jnp.int32)[:, None]).astype(
        jnp.float32
    )
    far_pick = (second_slot[None, :] == station_ids).astype(jnp.float32)
    gain_shard = (
        jnp.zeros((channels, ND, 2, owned), jnp.float32)
        .at[:, :, 0, :]
        .set(1.0)
        .reshape(channels, 2 * ND, owned)
    )
    all_gains = (
        jnp.zeros((channels, ND, 2, S), jnp.float32)
        .at[:, :, 0, :]
        .set(1.0)
        .reshape(channels, 2 * ND, S)
    )
    for iteration in range(ITERS):
        if iteration > 0:
            all_gains = lax.all_gather(gain_shard, "bl", axis=2, tiled=True)
        far_gain = lookup(all_gains.reshape(channels * 2 * ND, S), far_pick)
        near_gain = lookup(gain_shard.reshape(channels * 2 * ND, owned), near_pick)
        stacked = row_terms(model_vis, visible, far_gain, near_gain)
        station_terms = jnp.einsum(
            "fv,sv->fs",
            stacked,
            near_pick,
            precision=lax.Precision.HIGHEST,
            preferred_element_type=jnp.float32,
        )
        mine = station_terms.reshape(channels, 3 * ND, owned)
        sum_re = mine[:, :ND]
        sum_im = mine[:, ND : 2 * ND]
        sum_power = mine[:, 2 * ND :]
        gain_shard = update_gains(gain_shard, sum_re, sum_im, sum_power)
    return gain_shard


def solution(mesh):
    in_specs = (
        P(None, None, None, "ch"),
        P("bl", "ch"),
        P("bl"),
        P("ch", None, "bl"),
        P("ch", "bl"),
        P(None, "bl"),
        P(),
    )
    out_specs = P("ch", None, "bl")
    return jax.shard_map(body, mesh=mesh, in_specs=in_specs, out_specs=out_specs, check_vma=False)
```

profile of v0, /device:TPU:1, one launch (start us, length us, event | category | flops | bytes accessed | tf_op | source)
XLA Modules:
  0.0 517.9 jit_solution(18245494994774000052)
XLA Ops:
  6.5 1.6 copy-done
  8.1 2.4 fusion.41
  10.6 1.3 convert_bitcast_fusion
  11.9 2.6 copy.212
  14.5 0.7 copy-done.11
  15.2 1.4 copy.110
  16.5 13.1 %all-to-all-start.1 = ((s32[1,2,2048]{1,0,2:T(1,128)}), s32[1,2,2048]{1,0,2:T(1,128)S(1)}, u32[]{:S(2)}, u32[]{:S(2)}) async-start(s32[1,2,2048]{1,0,2:T(1,128)} %bitcast.7), calls=%async_computation.2 | async-start | bytes 2097152 | tf_op jit(solution)/shard_map/all_to_all | solution.py:112
  29.9 0.8 copy.116
  30.7 1.8 reshape.311
  32.5 2.4 scatter_custom_fusion
  35.0 23.2 %all-to-all-done.1 = s32[1,2,2048]{1,0,2:T(1,128)S(1)} async-done(((s32[1,2,2048]{1,0,2:T(1,128)}), s32[1,2,2048]{1,0,2:T(1,128)S(1)}, u32[]{:S(2)}, u32[]{:S(2)}) %all-to-all-start.1) | async-done | bytes 16416 | tf_op jit(solution)/shard_map/all_to_all | solution.py:112
  58.2 6.2 %all-to-all-start.2 = ((bf16[64,2,512]{2,1,0:T(2,128)(2,1)}), bf16[64,2,512]{2,1,0:T(2,128)(2,1)S(1)}, u32[]{:S(2)}, u32[]{:S(2)}) async-start(bf16[64,2,512]{2,1,0:T(2,128)(2,1)} %reshape.311), calls=%async_computation.3 | async-start | bytes 262144 | tf_op jit(solution)/shard_map/all_to_all | solution.py:111
  64.4 106.4 %slice_reduce_fusion = (s32[2048]{0:T(1024)S(1)}, s32[2048]{0:T(1024)S(1)}) fusion(s32[1,2,2048]{1,0,2:T(1,128)S(1)} %all-to-all-done.1), kind=kLoop, calls=%fused_computation.86 | loop fusion | bytes 32768 | tf_op jit(solution)/shard_map/slice | solution.py:114
  170.9 1.5 multiply_convert_fusion
  172.4 8.6 %copy.107 = bf16[16,16,2048]{1,0,2:T(8,128)(2,1)} copy(bf16[16,16,2048]{2,1,0:T(8,128)(2,1)S(1)} %multiply_convert_fusion) | data formatting | bytes 2097152 | tf_op jit(solution)/shard_map/convert_element_type | solution.py:102
  181.0 12.5 %reshape.309 = bf16[64,2,4096]{2,1,0:T(2,128)(2,1)} reshape(bf16[2048,16,16]{2,1,0:T(8,128)(2,1)} %bitcast.247) | data formatting | bytes 2097152
  193.4 10.7 %all-to-all-start = ((bf16[64,2,4096]{2,1,0:T(2,128)(2,1)}), bf16[64,2,4096]{2,1,0:T(2,128)(2,1)S(1)}, u32[]{:S(2)}, u32[]{:S(2)}) async-start(bf16[64,2,4096]{2,1,0:T(2,128)(2,1)} %reshape.309), calls=%async_computation.1 | async-start | bytes 2097152 | tf_op jit(solution)/shard_map/all_to_all | solution.py:110
  204.1 13.2 %gather_fusion.1 = s32[2048]{0:T(1024)S(1)} fusion(s32[512]{0:T(512)S(1)} %scatter_custom_fusion, s32[2048]{0:T(1024)S(1)} %broadcast_clamp_fusion), kind=kCustom, calls=%fused_computation.1 | custom fusion | bytes 24576 | tf_op jit(solution)/shard_map/gather | solution.py:114
  217.4 13.2 %gather_fusion = s32[2048]{0:T(1024)S(1)} fusion(s32[512]{0:T(512)S(1)} %scatter_custom_fusion, s32[2048]{0:T(1024)S(1)} %broadcast_clamp_fusion.1), kind=kCustom, calls=%fused_computation | custom fusion | bytes 24576 | tf_op jit(solution)/shard_map/gather | solution.py:115
  230.7 2.4 fusion.129
  233.0 3.4 fusion.8
  236.4 0.7 reshape.312
  237.1 2.3 fusion.168
  239.4 2.2 copy.203
  242.2 7.6 %reshape.310 = bf16[2048,16,16]{2,1,0:T(8,128)(2,1)} reshape(bf16[64,2,4096]{2,1,0:T(2,128)(2,1)S(1)} %all-to-all-done) | data formatting | bytes 2097152
  249.8 9.1 %copy.108 = bf16[16,16,2048]{2,0,1:T(8,128)(2,1)S(1)} copy(bf16[16,16,2048]{1,0,2:T(8,128)(2,1)} %bitcast.248) | data formatting | bytes 2097152 | tf_op jit(solution)/shard_map/all_to_all | solution.py:110
  259.0 1.5 copy-done.2
  260.5 2.9 subtract_reduce_fusion.3
  264.0 3.9 fusion.10
  268.3 1.3 collective-permute-start.1
  269.7 4.0 collective-permute-start
  274.7 56.0 %all_gather.9 = f32[16,16,512]{0,2,1:T(8,128)} all-gather(f32[16,16,8]{0,2,1:T(8,128)S(1)} %fusion.111), channel_id=1, replica_groups=mesh['bl'=64,'ch'=4] {'bl'}, dimensions={2}, use_global_device_ids=true | all-gather | bytes 532480 | tf_op jit(solution)/shard_map/all_gather | solution.py:135
  331.5 2.9 copy.176
  334.4 2.1 fusion.4
  336.5 0.9 fusion.127
  337.5 1.4 subtract_reduce_fusion.2
  338.9 1.5 copy.205
  340.4 1.5 copy.206
  342.3 3.9 fusion.16
  346.7 3.6 collective-permute-start.2
  350.6 1.3 collective-permute-start.3
  352.0 3.6 collective-permute-done.3
  355.7 53.5 %all_gather.10 = f32[16,16,512]{0,2,1:T(8,128)} all-gather(f32[16,16,8]{0,2,1:T(8,128)S(1)} %fusion.98), channel_id=1, replica_groups=mesh['bl'=64,'ch'=4] {'bl'}, dimensions={2}, use_global_device_ids=true | all-gather | bytes 532480 | tf_op jit(solution)/shard_map/all_gather | solution.py:135
  410.0 2.9 copy.180
  412.9 2.1 fusion.2
  414.9 0.9 fusion.125
  415.9 1.4 subtract_reduce_fusion.1
  417.4 1.5 copy.207
  418.8 1.5 copy.208
  420.8 3.9 fusion.22
  425.1 3.1 collective-permute-start.4
  428.5 1.3 collective-permute-start.5
  430.0 3.6 collective-permute-done.5
  433.6 53.5 %all_gather.11 = f32[16,16,512]{0,2,1:T(8,128)} all-gather(f32[16,16,8]{0,2,1:T(8,128)S(1)} %fusion.85), channel_id=1, replica_groups=mesh['bl'=64,'ch'=4] {'bl'}, dimensions={2}, use_global_device_ids=true | all-gather | bytes 532480 | tf_op jit(solution)/shard_map/all_gather | solution.py:135
  487.2 2.9 copy.184
  490.1 2.1 fusion.6
  492.2 1.0 fusion.123
  493.2 1.9 subtract_reduce_fusion
  495.4 1.8 multiply_add_fusion.1
  497.2 3.9 fusion.28
  501.6 3.1 collective-permute-start.6
  504.9 1.3 collective-permute-start.7
  506.4 3.6 collective-permute-done.7
  510.1 0.7 copy.170
  (116 shorter events, 8.4 us)
Async XLA Ops:
  6.5 1.6 copy-start
  6.5 4.0 copy-start.3
  6.5 164.3 %reduce-scatter.2.cloned.1.call-start = ((), (), s32[]{:S(2)}) async-start(), calls=%async_computation.4 | async-start | bytes 5242880 | tf_op jit(solution)/shard_map/reduce_scatter | solution.py:93
  14.5 0.7 copy-start.11
  14.5 15.2 %copy-start.19 = (s32[512]{0:T(512)S(1)}, s32[512]{0:T(512)}, u32[]{:S(2)}) copy-start(s32[512]{0:T(512)} %param.17) | copy-start | bytes 6148
  14.5 15.3 %copy-start.10 = (s32[16,2048]{1,0:T(8,128)S(1)}, s32[16,2048]{1,0:T(8,128)}, u32[]{:S(2)}) copy-start(s32[16,2048]{1,0:T(8,128)} %param.15) | copy-start | bytes 393220
  14.5 15.3 %copy-start.8 = (bf16[16,2,2048]{2,1,0:T(2,128)(2,1)S(1)}, bf16[16,2,2048]{2,1,0:T(2,128)(2,1)}, u32[]{:S(2)}) copy-start(bf16[16,2,2048]{2,1,0:T(2,128)(2,1)} %param.14) | copy-start | bytes 393220
  16.5 41.7 %all-to-all-start.1 = ((s32[1,2,2048]{1,0,2:T(1,128)}), s32[1,2,2048]{1,0,2:T(1,128)S(1)}, u32[]{:S(2)}, u32[]{:S(2)}) async-start(s32[1,2,2048]{1,0,2:T(1,128)} %bitcast.7), calls=%async_computation.2 | async-start | bytes 2097152 | tf_op jit(solution)/shard_map/all_to_all | solution.py:112
  29.9 244.7 %copy-start.12 = (f32[16]{0:T(128)}, f32[16]{0:T(128)S(1)}, u32[]{:S(2)}) copy-start(f32[16]{0:T(128)S(1)} %add_add_fusion) | copy-start | bytes 196
  58.2 135.2 %all-to-all-start.2 = ((bf16[64,2,512]{2,1,0:T(2,128)(2,1)}), bf16[64,2,512]{2,1,0:T(2,128)(2,1)S(1)}, u32[]{:S(2)}, u32[]{:S(2)}) async-start(bf16[64,2,512]{2,1,0:T(2,128)(2,1)} %reshape.311), calls=%async_computation.3 | async-start | bytes 262144 | tf_op jit(solution)/shard_map/all_to_all | solution.py:111
  193.4 48.7 %all-to-all-start = ((bf16[64,2,4096]{2,1,0:T(2,128)(2,1)}), bf16[64,2,4096]{2,1,0:T(2,128)(2,1)S(1)}, u32[]{:S(2)}, u32[]{:S(2)}) async-start(bf16[64,2,4096]{2,1,0:T(2,128)(2,1)} %reshape.309), calls=%async_computation.1 | async-start | bytes 2097152 | tf_op jit(solution)/shard_map/all_to_all | solution.py:110
  217.4 13.3 %copy-start.9 = (f32[16,8,2,8]{3,1,0,2:T(8,128)S(1)}, f32[16,8,2,8]{3,1,0,2:T(8,128)}, u32[]{:S(2)}) copy-start(f32[16,8,2,8]{3,1,0,2:T(8,128)} %constant.98) | copy-start | bytes 24580
  217.4 15.6 %copy-start.20 = (f32[16,8,2,512]{3,1,2,0:T(8,128)S(1)}, f32[16,8,2,512]{3,1,2,0:T(8,128)}, u32[]{:S(2)}) copy-start(f32[16,8,2,512]{3,1,2,0:T(8,128)} %constant.89.clone.1) | copy-start | bytes 1572868
  230.6 103.8 %copy-start.16 = (s32[2048]{0:T(1024)}, s32[2048]{0:T(1024)S(1)}, u32[]{:S(2)}) copy-start(s32[2048]{0:T(1024)S(1)} %gather_fusion) | copy-start | bytes 24580
  258.9 1.6 copy-start.2
  268.3 6.3 %collective-permute-start.1 = (f32[1,16,8]{0,2,1:T(8,128)S(1)}, f32[1,16,8]{0,2,1:T(8,128)S(1)}, u32[]{:S(2)}, u32[]{:S(2)}) collective-permute-start(f32[1,16,8]{0,2,1:T(8,128)S(1)} %copy.127), channel_id=1, source_target_pairs={{1,0},{2,1},{3,2},{5,4},{6,5},{7,6},{9,8},{10,9},{11,10},{13,12},{... | collective-permute-start | bytes 1544 | tf_op jit(solution)/shard_map/ppermute | solution.py:19
  269.7 4.8 collective-permute-start
  342.3 4.0 copy-start.4
  342.3 4.0 copy-start.6
  342.3 13.2 %copy-start.13 = (f32[16]{0:T(128)S(1)}, f32[16]{0:T(128)}, u32[]{:S(2)}) copy-start(f32[16]{0:T(128)} %copy-done.12) | copy-start | bytes 196
  346.7 5.3 %collective-permute-start.2 = (f32[1,16,8]{0,2,1:T(8,128)S(1)}, f32[1,16,8]{0,2,1:T(8,128)S(1)}, u32[]{:S(2)}, u32[]{:S(2)}) collective-permute-start(f32[1,16,8]{0,2,1:T(8,128)S(1)} %copy.138), channel_id=1, source_target_pairs={{0,1},{1,2},{2,3},{4,5},{5,6},{6,7},{8,9},{9,10},{10,11},{12,13},{... | collective-permute-start | bytes 1544 | tf_op jit(solution)/shard_map/ppermute | solution.py:18
  350.6 5.0 collective-permute-start.3
  409.2 3.6 copy-start.17
  420.7 4.0 copy-start.5
  420.8 4.0 copy-start.7
  420.8 12.7 %copy-start.14 = (f32[16]{0:T(128)S(1)}, f32[16]{0:T(128)}, u32[]{:S(2)}) copy-start(f32[16]{0:T(128)} %copy-done.12) | copy-start | bytes 196
  425.1 4.8 collective-permute-start.4
  428.5 5.0 collective-permute-start.5
  487.1 3.0 copy-start.18
  495.4 15.4 %copy-start.1 = (bf16[4,64,16,256]{3,2,1,0:T(8,128)(2,1)S(1)}, bf16[4,64,16,256]{3,2,1,0:T(8,128)(2,1)}, u32[]{:S(2)}) copy-start(bf16[4,64,16,256]{3,2,1,0:T(8,128)(2,1)} %param.11) | copy-start | bytes 6291460
  497.2 12.7 %copy-start.15 = (f32[16]{0:T(128)S(1)}, f32[16]{0:T(128)}, u32[]{:S(2)}) copy-start(f32[16]{0:T(128)} %copy-done.12) | copy-start | bytes 196
  501.6 4.8 collective-permute-start.6
  504.9 5.0 collective-permute-start.7
Sparse Core Ops, SparseCore 0:
  14.6 53.0 reduce-scatter.1
where the time goes:
time: 525 us; the launch traced here: 518 us
  local copies, waits for them, and re-layouts  209 us (40%)
  blocking collectives  163 us (31%)
  starting transfers between devices  49 us (9%)
  waiting for transfers between devices  34.6 us (7%)
  matrix products  34.3 us (7%)
  between operations  14.5 us (3%)
  other arithmetic  13.8 us (3%)
    all_gather x3, blocking collectives, body(): all_gains = lax.all_gather(gain_shard, 'bl', axis=2, tiled=True)  163 us
    slice x1, local copies, waits for them, and re-layouts, body(): first_slot = inverse[packed[0, 0]]  106 us
    unnamed x55, local copies, waits for them, and re-layouts  36.5 us
    all_to_all x1, waiting for transfers between devices, body(): lax.all_to_all(packed, 'bl', split_axis=2, concat_axis=2, tiled=True)  23.2 us
    dot_general x4, matrix products, body(): jnp.einsum('fv,sv->fs', stacked, near_pick, precision=lax.Precision.HIGHE...  15.8 us
    dot_general x8, matrix products, lookup(): jnp.dot(gain_flat, pick, precision=lax.Precision.HIGHEST, preferred_eleme...  14.9 us
    ppermute x4, starting transfers between devices, extended(): before = lax.ppermute(last, axis, up)  13.8 us
    gather x1, local copies, waits for them, and re-layouts, body(): first_slot = inverse[packed[0, 0]]  13.2 us
  transfers between devices with their start and end apart: 12, of which 5 were waited for; matrix products, arithmetic and copies ran while one was open for 34% of the time, Pallas kernels for 0%

commit v1 on v0

--- a/solution.py
+++ b/solution.py
@@ -132,7 +132,7 @@
     )
     for iteration in range(ITERS):
         if iteration > 0:
-            all_gains = lax.all_gather(gain_shard, "bl", axis=2, tiled=True)
+            all_gains = jnp.concatenate(lax.all_gather(gain_shard, "bl"), axis=2)
         far_gain = lookup(all_gains.reshape(channels * 2 * ND, S), far_pick)
         near_gain = lookup(gain_shard.reshape(channels * 2 * ND, owned), near_pick)
         stacked = row_terms(model_vis, visible, far_gain, near_gain)

time: 525 us -> 554 us (1.055)
  local copies, waits for them, and re-layouts: 209 us -> 227 us
  blocking collectives: 163 us -> 173 us
    reshape x0 -> x3, local copies, waits for them, and re-layouts: none -> 18 us  [body(): all_gains = jnp.concatenate(lax.all_gather(gain_shard, 'bl'), axis=2)]
    all_gather x3, blocking collectives: 163 us -> 173 us  [body(): all_gains = jnp.concatenate(lax.all_gather(gain_shard, 'bl'), axis=2)]
  transfers between devices with their start and end apart: 12 -> 12, of which waited for: 5 -> 5; matrix products, arithmetic and copies ran while one was open for 34% -> 32% of each run, Pallas kernels for 0% -> 0%
where the time goes in v1:
time: 554 us; the launch traced here: 547 us
  local copies, waits for them, and re-layouts  227 us (41%)
  blocking collectives  173 us (31%)
  starting transfers between devices  49.4 us (9%)
  waiting for transfers between devices  34.6 us (6%)
  matrix products  34.3 us (6%)
  between operations  14.7 us (3%)
  other arithmetic  13.8 us (2%)
    all_gather x3, blocking collectives, body(): all_gains = jnp.concatenate(lax.all_gather(gain_shard, 'bl'), axis=2)  173 us
    slice x1, local copies, waits for them, and re-layouts, body(): first_slot = inverse[packed[0, 0]]  107 us
    unnamed x55, local copies, waits for them, and re-layouts  36.5 us
    all_to_all x1, waiting for transfers between devices, body(): lax.all_to_all(packed, 'bl', split_axis=2, concat_axis=2, tiled=True)  23.2 us
    reshape x3, local copies, waits for them, and re-layouts, body(): all_gains = jnp.concatenate(lax.all_gather(gain_shard, 'bl'), axis=2)  18 us
    dot_general x4, matrix products, body(): jnp.einsum('fv,sv->fs', stacked, near_pick, precision=lax.Precision.HIGHE...  15.8 us
    dot_general x8, matrix products, lookup(): jnp.dot(gain_flat, pick, precision=lax.Precision.HIGHEST, preferred_eleme...  14.9 us
    ppermute x4, starting transfers between devices, extended(): before = lax.ppermute(last, axis, up)  14.1 us
  transfers between devices with their start and end apart: 12, of which 5 were waited for; matrix products, arithmetic and copies ran while one was open for 32% of the time, Pallas kernels for 0%

profile of v1, /device:TPU:1, one launch (start us, length us, event | category | flops | bytes accessed | tf_op | source)
XLA Modules:
  0.0 546.7 jit_solution(202826126808680573)
XLA Ops:
  6.5 1.6 copy-done
  8.1 2.4 fusion.41
  10.6 1.3 convert_bitcast_fusion
  11.9 2.6 copy.279
  15.2 1.4 copy.171
  16.5 13.1 %all-to-all-start.1 = ((s32[1,2,2048]{1,0,2:T(1,128)}), s32[1,2,2048]{1,0,2:T(1,128)S(1)}, u32[]{:S(2)}, u32[]{:S(2)}) async-start(s32[1,2,2048]{1,0,2:T(1,128)} %bitcast.7), calls=%async_computation.2 | async-start | bytes 2097152 | tf_op jit(solution)/shard_map/all_to_all | solution.py:112
  29.9 0.8 copy.177
  30.7 1.8 reshape.323
  32.5 2.4 scatter_custom_fusion
  35.0 23.2 %all-to-all-done.1 = s32[1,2,2048]{1,0,2:T(1,128)S(1)} async-done(((s32[1,2,2048]{1,0,2:T(1,128)}), s32[1,2,2048]{1,0,2:T(1,128)S(1)}, u32[]{:S(2)}, u32[]{:S(2)}) %all-to-all-start.1) | async-done | bytes 16416 | tf_op jit(solution)/shard_map/all_to_all | solution.py:112
  58.2 6.2 %all-to-all-start.2 = ((bf16[64,2,512]{2,1,0:T(2,128)(2,1)}), bf16[64,2,512]{2,1,0:T(2,128)(2,1)S(1)}, u32[]{:S(2)}, u32[]{:S(2)}) async-start(bf16[64,2,512]{2,1,0:T(2,128)(2,1)} %reshape.323), calls=%async_computation.3 | async-start | bytes 262144 | tf_op jit(solution)/shard_map/all_to_all | solution.py:111
  64.4 106.6 %slice_reduce_fusion = (s32[2048]{0:T(1024)S(1)}, s32[2048]{0:T(1024)S(1)}) fusion(s32[1,2,2048]{1,0,2:T(1,128)S(1)} %all-to-all-done.1), kind=kLoop, calls=%fused_computation.86 | loop fusion | bytes 32768 | tf_op jit(solution)/shard_map/slice | solution.py:114
  171.0 1.5 multiply_convert_fusion
  172.6 8.6 %copy.168 = bf16[16,16,2048]{1,0,2:T(8,128)(2,1)} copy(bf16[16,16,2048]{2,1,0:T(8,128)(2,1)S(1)} %multiply_convert_fusion) | data formatting | bytes 2097152 | tf_op jit(solution)/shard_map/convert_element_type | solution.py:102
  181.2 12.5 %reshape.321 = bf16[64,2,4096]{2,1,0:T(2,128)(2,1)} reshape(bf16[2048,16,16]{2,1,0:T(8,128)(2,1)} %bitcast.259) | data formatting | bytes 2097152
  193.6 10.8 %all-to-all-start = ((bf16[64,2,4096]{2,1,0:T(2,128)(2,1)}), bf16[64,2,4096]{2,1,0:T(2,128)(2,1)S(1)}, u32[]{:S(2)}, u32[]{:S(2)}) async-start(bf16[64,2,4096]{2,1,0:T(2,128)(2,1)} %reshape.321), calls=%async_computation.1 | async-start | bytes 2097152 | tf_op jit(solution)/shard_map/all_to_all | solution.py:110
  204.5 13.2 %gather_fusion.1 = s32[2048]{0:T(1024)S(1)} fusion(s32[512]{0:T(512)S(1)} %scatter_custom_fusion, s32[2048]{0:T(1024)S(1)} %broadcast_clamp_fusion), kind=kCustom, calls=%fused_computation.1 | custom fusion | bytes 24576 | tf_op jit(solution)/shard_map/gather | solution.py:114
  217.8 13.2 %gather_fusion = s32[2048]{0:T(1024)S(1)} fusion(s32[512]{0:T(512)S(1)} %scatter_custom_fusion, s32[2048]{0:T(1024)S(1)} %broadcast_clamp_fusion.1), kind=kCustom, calls=%fused_computation | custom fusion | bytes 24576 | tf_op jit(solution)/shard_map/gather | solution.py:115
  231.0 2.4 fusion.129
  233.4 3.4 fusion.8
  237.5 2.3 fusion.168
  239.8 2.2 copy.270
  242.5 7.6 %reshape.322 = bf16[2048,16,16]{2,1,0:T(8,128)(2,1)} reshape(bf16[64,2,4096]{2,1,0:T(2,128)(2,1)S(1)} %all-to-all-done) | data formatting | bytes 2097152
  250.1 9.1 %copy.169 = bf16[16,16,2048]{2,0,1:T(8,128)(2,1)S(1)} copy(bf16[16,16,2048]{1,0,2:T(8,128)(2,1)} %bitcast.260) | data formatting | bytes 2097152 | tf_op jit(solution)/shard_map/all_to_all | solution.py:110
  259.4 1.5 copy-done.2
  260.9 2.9 subtract_reduce_fusion.3
  264.3 3.9 fusion.10
  268.7 1.3 collective-permute-start.1
  270.0 4.0 collective-permute-start
  275.9 59.1 %all-gather = f32[1024,16,8]{1,2,0:T(8,128)} all-gather(f32[16,16,8]{1,2,0:T(8,128)S(1)} %copy.190), channel_id=2, replica_groups=mesh['bl'=64,'ch'=4] {'bl'}, dimensions={0}, use_global_device_ids=true | all-gather | bytes 532480 | tf_op jit(solution)/shard_map/all_gather | solution.py:135
  335.0 6.0 %copy.192 = f32[16,16,64,8]{0,3,2,1:T(8,128)} copy(f32[16,16,64,8]{1,3,0,2:T(8,128)} %bitcast.262) | data formatting | bytes 1048576 | tf_op jit(solution)/shard_map/reshape | solution.py:135
  341.0 2.9 copy.243
  343.9 2.1 fusion.4
  346.0 1.0 fusion.127
  347.0 1.4 subtract_reduce_fusion.2
  348.4 1.5 copy.272
  349.9 1.5 copy.273
  351.8 3.9 fusion.16
  356.2 3.9 collective-permute-start.2
  360.3 1.3 collective-permute-start.3
  361.8 3.6 collective-permute-done.3
  366.3 57.0 %all-gather.1 = f32[1024,16,8]{1,2,0:T(8,128)} all-gather(f32[16,16,8]{1,2,0:T(8,128)S(1)} %copy.206), channel_id=3, replica_groups=mesh['bl'=64,'ch'=4] {'bl'}, dimensions={0}, use_global_device_ids=true | all-gather | bytes 532480 | tf_op jit(solution)/shard_map/all_gather | solution.py:135
  423.3 6.0 %copy.208 = f32[16,16,64,8]{0,3,2,1:T(8,128)} copy(f32[16,16,64,8]{1,3,0,2:T(8,128)} %bitcast.264) | data formatting | bytes 1048576 | tf_op jit(solution)/shard_map/reshape | solution.py:135
  429.3 2.9 copy.247
  432.2 2.1 fusion.2
  434.3 1.0 fusion.125
  435.3 1.4 subtract_reduce_fusion.1
  436.7 1.5 copy.274
  438.2 1.5 copy.275
  440.2 3.9 fusion.22
  444.5 3.1 collective-permute-start.4
  447.9 1.3 collective-permute-start.5
  449.3 3.6 collective-permute-done.5
  453.2 56.7 %all-gather.2 = f32[1024,16,8]{1,2,0:T(8,128)} all-gather(f32[16,16,8]{1,2,0:T(8,128)S(1)} %copy.222), channel_id=4, replica_groups=mesh['bl'=64,'ch'=4] {'bl'}, dimensions={0}, use_global_device_ids=true | all-gather | bytes 532480 | tf_op jit(solution)/shard_map/all_gather | solution.py:135
  509.9 6.0 %copy.224 = f32[16,16,64,8]{0,3,2,1:T(8,128)} copy(f32[16,16,64,8]{1,3,0,2:T(8,128)} %bitcast.266) | data formatting | bytes 1048576 | tf_op jit(solution)/shard_map/reshape | solution.py:135
  515.9 2.9 copy.251
  518.8 2.1 fusion.6
  520.9 1.0 fusion.123
  521.8 1.9 subtract_reduce_fusion
  524.0 1.8 multiply_add_fusion.1
  525.9 3.9 fusion.28
  530.2 3.1 collective-permute-start.6
  533.6 1.3 collective-permute-start.7
  535.0 3.6 collective-permute-done.7
  (122 shorter events, 10.8 us)
Async XLA Ops:
  6.5 1.6 copy-start
  6.5 4.0 copy-start.3
  6.5 164.5 %reduce-scatter.2.cloned.1.call-start = ((), (), s32[]{:S(2)}) async-start(), calls=%async_computation.4 | async-start | bytes 5242880 | tf_op jit(solution)/shard_map/reduce_scatter | solution.py:93
  14.5 0.7 copy-start.11
  14.5 15.2 %copy-start.19 = (s32[512]{0:T(512)S(1)}, s32[512]{0:T(512)}, u32[]{:S(2)}) copy-start(s32[512]{0:T(512)} %param.17) | copy-start | bytes 6148
  14.5 15.3 %copy-start.10 = (s32[16,2048]{1,0:T(8,128)S(1)}, s32[16,2048]{1,0:T(8,128)}, u32[]{:S(2)}) copy-start(s32[16,2048]{1,0:T(8,128)} %param.15) | copy-start | bytes 393220
  14.5 15.3 %copy-start.8 = (bf16[16,2,2048]{2,1,0:T(2,128)(2,1)S(1)}, bf16[16,2,2048]{2,1,0:T(2,128)(2,1)}, u32[]{:S(2)}) copy-start(bf16[16,2,2048]{2,1,0:T(2,128)(2,1)} %param.14) | copy-start | bytes 393220
  16.5 41.7 %all-to-all-start.1 = ((s32[1,2,2048]{1,0,2:T(1,128)}), s32[1,2,2048]{1,0,2:T(1,128)S(1)}, u32[]{:S(2)}, u32[]{:S(2)}) async-start(s32[1,2,2048]{1,0,2:T(1,128)} %bitcast.7), calls=%async_computation.2 | async-start | bytes 2097152 | tf_op jit(solution)/shard_map/all_to_all | solution.py:112
  29.9 245.0 %copy-start.12 = (f32[16]{0:T(128)}, f32[16]{0:T(128)S(1)}, u32[]{:S(2)}) copy-start(f32[16]{0:T(128)S(1)} %add_add_fusion) | copy-start | bytes 196
  58.2 135.4 %all-to-all-start.2 = ((bf16[64,2,512]{2,1,0:T(2,128)(2,1)}), bf16[64,2,512]{2,1,0:T(2,128)(2,1)S(1)}, u32[]{:S(2)}, u32[]{:S(2)}) async-start(bf16[64,2,512]{2,1,0:T(2,128)(2,1)} %reshape.323), calls=%async_computation.3 | async-start | bytes 262144 | tf_op jit(solution)/shard_map/all_to_all | solution.py:111
  193.6 48.9 %all-to-all-start = ((bf16[64,2,4096]{2,1,0:T(2,128)(2,1)}), bf16[64,2,4096]{2,1,0:T(2,128)(2,1)S(1)}, u32[]{:S(2)}, u32[]{:S(2)}) async-start(bf16[64,2,4096]{2,1,0:T(2,128)(2,1)} %reshape.321), calls=%async_computation.1 | async-start | bytes 2097152 | tf_op jit(solution)/shard_map/all_to_all | solution.py:110
  217.7 13.3 %copy-start.9 = (f32[16,8,2,8]{3,1,0,2:T(8,128)S(1)}, f32[16,8,2,8]{3,1,0,2:T(8,128)}, u32[]{:S(2)}) copy-start(f32[16,8,2,8]{3,1,0,2:T(8,128)} %constant.98) | copy-start | bytes 24580
  217.8 15.6 %copy-start.20 = (f32[16,8,2,512]{3,1,2,0:T(8,128)S(1)}, f32[16,8,2,512]{3,1,2,0:T(8,128)}, u32[]{:S(2)}) copy-start(f32[16,8,2,512]{3,1,2,0:T(8,128)} %constant.89.clone.1) | copy-start | bytes 1572868
  231.0 112.9 %copy-start.16 = (s32[2048]{0:T(1024)}, s32[2048]{0:T(1024)S(1)}, u32[]{:S(2)}) copy-start(s32[2048]{0:T(1024)S(1)} %gather_fusion) | copy-start | bytes 24580
  259.3 1.6 copy-start.2
  268.7 6.3 %collective-permute-start.1 = (f32[1,16,8]{0,2,1:T(8,128)S(1)}, f32[1,16,8]{0,2,1:T(8,128)S(1)}, u32[]{:S(2)}, u32[]{:S(2)}) collective-permute-start(f32[1,16,8]{0,2,1:T(8,128)S(1)} %copy.188), channel_id=1, source_target_pairs={{1,0},{2,1},{3,2},{5,4},{6,5},{7,6},{9,8},{10,9},{11,10},{13,12},{... | collective-permute-start | bytes 1544 | tf_op jit(solution)/shard_map/ppermute | solution.py:19
  270.0 4.8 collective-permute-start
  351.8 4.0 copy-start.4
  351.8 4.0 copy-start.6
  351.8 13.5 %copy-start.13 = (f32[16]{0:T(128)S(1)}, f32[16]{0:T(128)}, u32[]{:S(2)}) copy-start(f32[16]{0:T(128)} %copy-done.12) | copy-start | bytes 196
  356.2 5.6 %collective-permute-start.2 = (f32[1,16,8]{0,2,1:T(8,128)S(1)}, f32[1,16,8]{0,2,1:T(8,128)S(1)}, u32[]{:S(2)}, u32[]{:S(2)}) collective-permute-start(f32[1,16,8]{0,2,1:T(8,128)S(1)} %copy.201), channel_id=1, source_target_pairs={{0,1},{1,2},{2,3},{4,5},{5,6},{6,7},{8,9},{9,10},{10,11},{12,13},{... | collective-permute-start | bytes 1544 | tf_op jit(solution)/shard_map/ppermute | solution.py:18
  360.3 5.0 collective-permute-start.3
  429.3 2.9 copy-start.17
  440.1 4.0 copy-start.5
  440.1 4.0 copy-start.7
  440.1 12.7 %copy-start.14 = (f32[16]{0:T(128)S(1)}, f32[16]{0:T(128)}, u32[]{:S(2)}) copy-start(f32[16]{0:T(128)} %copy-done.12) | copy-start | bytes 196
  444.5 4.8 collective-permute-start.4
  447.9 5.0 collective-permute-start.5
  515.9 2.9 copy-start.18
  524.0 15.4 %copy-start.1 = (bf16[4,64,16,256]{3,2,1,0:T(8,128)(2,1)S(1)}, bf16[4,64,16,256]{3,2,1,0:T(8,128)(2,1)}, u32[]{:S(2)}) copy-start(bf16[4,64,16,256]{3,2,1,0:T(8,128)(2,1)} %param.11) | copy-start | bytes 6291460
  525.9 12.7 %copy-start.15 = (f32[16]{0:T(128)S(1)}, f32[16]{0:T(128)}, u32[]{:S(2)}) copy-start(f32[16]{0:T(128)} %copy-done.12) | copy-start | bytes 196
  530.2 4.8 collective-permute-start.6
  533.6 5.0 collective-permute-start.7
Sparse Core Ops, SparseCore 0:
  14.6 53.0 reduce-scatter.1
